TPU v7x, 32 devices: a whole 2x2x4 slice. The times are simulated.
32 devices in a mesh: lon: 8 (over z, x), lat: 4 (over y, core).
Axes of the slice: x: 2, y: 2, z: 4, core: 2. Of those that a mesh axis runs over, the one named last changes fastest.
Arguments:
- increment: bfloat16 [256, 512, 128], P('lon', 'lat'), may hold values from -6 to 6
- jacobian: bfloat16 [512, 128, 3072], P(('lon', 'lat')), may hold values from -0.0625 to 0.0625
- lat_weight: float32 [512, 8], P(('lon', 'lat')), may hold values from 0.2 to 2
- centre: int32 [512], P(('lon', 'lat')), may hold values from 0 to 31
- west: int32 [512], P(('lon', 'lat')), may hold values from 0 to 32
- east: int32 [512], P(('lon', 'lat')), may hold values from 0 to 32
- lat_offset: int32 [512], P(('lon', 'lat')), may hold values from 0 to 504
- lev_offset: int32 [512], P(('lon', 'lat')), may hold values from 0 to 96
Outputs:
- departures: float32 [512, 128], P(('lon', 'lat'))
All inputs are finite; a program needn't handle non-finite values.
Results may differ from a plain program's by a relative error of at most 0.0029.
Values may be sent and summed in bfloat16 or wider, within the bound.
A program may use at most 128 MiB of HBM per device.

v0:
```python
import jax
import jax.numpy as jnp
from jax import lax
from jax.sharding import PartitionSpec as P

BLAT = 8
BLEV = 32


def padded(block, sides, width):
    for axis, dim in sides:
        count = lax.axis_size(axis)
        forward = [(i, i + 1) for i in range(count - 1)]
        forward.append((count - 1, 0))
        backward = [(target, source) for source, target in forward]
        low = lax.ppermute(
            lax.slice_in_dim(block, block.shape[dim] - width, None, axis=dim), axis, forward
        )
        high = lax.ppermute(lax.slice_in_dim(block, 0, width, axis=dim), axis, backward)
        block = jnp.concatenate([low, block, high], axis=dim)
    return block


def shifted(block, axis, distance):
    devices = range(lax.axis_size(axis))
    route = [((i - distance) % len(devices), i) for i in devices]
    return lax.ppermute(block, axis, route)


def local(increment, jacobian, lat_weight, centre, west, east, lat_offset, lev_offset):
    width = increment.shape[0]
    span = 3 * width
    slots = centre.shape[0]
    band = lax.axis_index("lat")
    band_count = lax.axis_size("lat")
    rows_band = increment.shape[1]
    packed = jnp.concatenate(
        [
            lat_weight,
            lat_offset[:, None].astype(jnp.float32),
            lev_offset[:, None].astype(jnp.float32),
        ],
        axis=1,
    )
    packed_all = lax.all_gather(packed, "lat", axis=0, tiled=True)
    nearby = padded(packed_all[None], (("lon", 0),), 1)
    listed = nearby.reshape(3 * band_count * slots, BLAT + 2)
    weights = listed[:, :BLAT]
    lat_first = listed[:, BLAT].astype(jnp.int32)
    lev_first = listed[:, BLAT + 1].astype(jnp.int32)
    local_rows = lat_first[:, None] + jnp.arange(BLAT, dtype=jnp.int32)[None, :] - band * rows_band
    selector = (
        local_rows[:, :, None] == jnp.arange(rows_band, dtype=jnp.int32)[None, None, :]
    ).astype(jnp.float32)
    row_weight = jnp.einsum("nj,nji->ni", weights, selector, precision=lax.Precision.HIGHEST)
    lifted = jnp.einsum(
        "ni,cik->nck", row_weight, increment.astype(jnp.float32), precision=lax.Precision.HIGHEST
    )

    def level_box(column_block, first):
        return lax.dynamic_slice_in_dim(column_block, first, BLEV, 1)

    partial_value = jax.vmap(level_box)(lifted, lev_first).reshape(
        3, band_count, slots, width, BLEV
    )
    summed = lax.psum_scatter(partial_value, "lat", scatter_dimension=1, tiled=True)[:, 0]
    pieces = summed.astype(jnp.bfloat16)
    from_east = shifted(pieces[0], "lon", -1)
    from_west = shifted(pieces[2], "lon", 1)
    profile = jnp.concatenate([from_west, pieces[1], from_east], axis=1)
    rows = jnp.arange(span, dtype=jnp.int32)[None, :]
    keep = (rows >= width + centre[:, None] - west[:, None]) & (
        rows <= width + centre[:, None] + east[:, None]
    )
    profile = jnp.where(keep[:, :, None], profile, jnp.zeros_like(profile))
    flat_profile = profile.reshape(slots, span * BLEV)
    return jnp.einsum("str,sr->st", jacobian, flat_profile, preferred_element_type=jnp.float32)


def solution(mesh):
    return jax.shard_map(
        local,
        mesh=mesh,
        in_specs=(
            P("lon", "lat", None),
            P(("lon", "lat"), None, None),
            P(("lon", "lat"), None),
            P(("lon", "lat")),
            P(("lon", "lat")),
            P(("lon", "lat")),
            P(("lon", "lat")),
            P(("lon", "lat")),
        ),
        out_specs=P(("lon", "lat"), None),
        check_vma=False,
    )
```

profile of v0, /device:TPU:0, one launch (start us, length us, event | category | flops | bytes accessed | tf_op | source)
XLA Modules:
  0.0 128.4 jit_solution(14367757345197577358)
XLA Ops:
  0.0 0.7 convert_bitcast_fusion.1
  0.7 0.7 convert_bitcast_fusion
  1.6 0.8 copy.25
  2.4 6.2 %all_gather.3 = f32[64,10]{1,0:T(8,128)S(1)} all-gather(f32[16,10]{1,0:T(8,128)S(1)} %pad_maximum_fusion.1), channel_id=1, replica_groups=mesh['lon'=8,'lat'=4] {'lat'}, dimensions={0}, use_global_device_ids=true | all-gather | bytes 3200 | tf_op jit(solution)/shard_map/all_gather | solution.py:45
  8.6 5.0 %collective-permute-start.1 = (f32[1,64,10]{2,1,0:T(8,128)S(1)}, f32[1,64,10]{2,1,0:T(8,128)S(1)}, u32[]{:S(2)}, u32[]{:S(2)}) collective-permute-start(f32[1,64,10]{2,1,0:T(8,128)S(1)} %bitcast.35), channel_id=1, source_target_pairs={{4,0},{8,4},{12,8},{16,12},{20,16},{24,20},{28,24},{0,28},{5,1},{9... | collective-permute-start | bytes 7688 | tf_op jit(solution)/shard_map/ppermute | solution.py:19
  13.6 0.7 add_subtract_fusion.1
  14.4 1.2 dynamic-slice
  15.7 4.5 %collective-permute-done = f32[1,64,10]{2,1,0:T(8,128)S(1)} collective-permute-done((f32[1,64,10]{2,1,0:T(8,128)S(1)}, f32[1,64,10]{2,1,0:T(8,128)S(1)}, u32[]{:S(2)}, u32[]{:S(2)}) %collective-permute-start) | collective-permute-done | bytes 2592 | tf_op jit(solution)/shard_map/ppermute | solution.py:16
  20.6 0.8 fusion
  21.5 3.0 %fusion.6 = f32[192,32,128]{2,0,1:T(8,128)} fusion(f32[192,128,1]{1,0,2:T(8,128)S(1)} %bitcast.38, bf16[32,128,128]{2,1,0:T(8,128)(2,1)S(1)} %copy-done), kind=kOutput, calls=%fused_computation.26 | convolution fusion | flops 1207959552 | bytes 4292608 | tf_op jit(solution)/shard_map/ni,cik->nck/dot_general | solution.py:56
  24.5 11.5 %copy.31 = f32[192,32,128]{1,0,2:T(8,128)} copy(f32[192,32,128]{2,0,1:T(8,128)} %fusion.6) | data formatting | bytes 6291456 | tf_op jit(solution)/shard_map/ni,cik->nck/dot_general | solution.py:56
  36.1 13.1 %gather_fusion = f32[192,32,32]{1,0,2:T(8,128)} fusion(f32[192,32,128]{1,0,2:T(8,128)} %copy.31, s32[192]{0:T(256)S(1)} %bitcast.34), kind=kCustom, calls=%fused_computation | custom fusion | bytes 1575168 | tf_op jit(solution)/shard_map/vmap()/gather | solution.py:61
  49.1 4.0 %copy.32 = f32[3,4,16,32,32]{4,3,2,1,0:T(8,128)} copy(f32[3,4,16,32,32]{3,2,1,0,4:T(8,128)} %bitcast.33) | data formatting | bytes 1572864 | tf_op jit(solution)/shard_map/reshape | solution.py:63
  53.1 58.3 %all-reduce.3 = bf16[3,4,16,32,32]{4,3,2,1,0:T(8,128)(2,1)S(1)} all-reduce(f32[3,4,16,32,32]{4,3,2,1,0:T(8,128)} %copy.32), channel_id=2, replica_groups=mesh['lon'=8,'lat'=4] {'lat'}, use_global_device_ids=true, to_apply=%region_0.0.clone | all-reduce | flops 196608 | bytes 1179648
  111.5 0.7 dynamic-slice_convert_fusion
  112.3 4.7 %collective-permute-start.3 = (bf16[16,32,32]{2,1,0:T(8,128)(2,1)S(1)}, bf16[16,32,32]{2,1,0:T(8,128)(2,1)S(1)}, u32[]{:S(2)}, u32[]{:S(2)}) collective-permute-start(bf16[16,32,32]{2,1,0:T(8,128)(2,1)S(1)} %get-tuple-element.6), channel_id=1, source_target_pairs={{4,0},{8,4},{12,8},{16,12},{20,16},{24,20},{28,24},{0,28},{5,1},{9... | collective-permute-start | bytes 98312 | tf_op jit(solution)/shard_map/ppermute | solution.py:27
  117.0 0.1 copy.34
  117.2 3.4 %collective-permute-done.2 = bf16[16,32,32]{2,1,0:T(8,128)(2,1)S(1)} collective-permute-done((bf16[16,32,32]{2,1,0:T(8,128)(2,1)S(1)}, bf16[16,32,32]{2,1,0:T(8,128)(2,1)S(1)}, u32[]{:S(2)}, u32[]{:S(2)}) %collective-permute-start.2) | collective-permute-done | bytes 32800 | tf_op jit(solution)/shard_map/ppermute | solution.py:27
  120.5 0.1 copy.33
  120.7 0.1 copy.35
  120.8 0.1 maximum_select_fusion
  121.0 0.2 copy.36
  121.2 0.2 reshape.103
  121.4 7.0 %fusion.7 = f32[16,1,128]{2,1,0:T(1,128)} fusion(bf16[16,3072,1]{1,2,0:T(2,128)(2,1)S(1)} %reshape.103, bf16[16,128,3072]{2,1,0:T(8,128)(2,1)} %param.9), kind=kOutput, calls=%fused_computation.27 | convolution fusion | flops 12582912 | bytes 12689408 | tf_op jit(solution)/shard_map/str,sr->st/dot_general | solution.py:77
  (21 shorter events, 1.0 us)
Async XLA Ops:
  0.0 21.5 %copy-start = (bf16[32,128,128]{2,1,0:T(8,128)(2,1)S(1)}, bf16[32,128,128]{2,1,0:T(8,128)(2,1)}, u32[]{:S(2)}) copy-start(bf16[32,128,128]{2,1,0:T(8,128)(2,1)} %param.8) | copy-start | bytes 3145732
  8.6 7.0 %collective-permute-start.1 = (f32[1,64,10]{2,1,0:T(8,128)S(1)}, f32[1,64,10]{2,1,0:T(8,128)S(1)}, u32[]{:S(2)}, u32[]{:S(2)}) collective-permute-start(f32[1,64,10]{2,1,0:T(8,128)S(1)} %bitcast.35), channel_id=1, source_target_pairs={{4,0},{8,4},{12,8},{16,12},{20,16},{24,20},{28,24},{0,28},{5,1},{9... | collective-permute-start | bytes 7688 | tf_op jit(solution)/shard_map/ppermute | solution.py:19
  13.6 6.6 %collective-permute-start = (f32[1,64,10]{2,1,0:T(8,128)S(1)}, f32[1,64,10]{2,1,0:T(8,128)S(1)}, u32[]{:S(2)}, u32[]{:S(2)}) collective-permute-start(f32[1,64,10]{2,1,0:T(8,128)S(1)} %bitcast.36), channel_id=1, source_target_pairs={{0,4},{4,8},{8,12},{12,16},{16,20},{20,24},{24,28},{28,0},{1,5},{5... | collective-permute-start | bytes 7688 | tf_op jit(solution)/shard_map/ppermute | solution.py:16
  112.2 8.3 %collective-permute-start.2 = (bf16[16,32,32]{2,1,0:T(8,128)(2,1)S(1)}, bf16[16,32,32]{2,1,0:T(8,128)(2,1)S(1)}, u32[]{:S(2)}, u32[]{:S(2)}) collective-permute-start(bf16[16,32,32]{2,1,0:T(8,128)(2,1)S(1)} %get-tuple-element.5), channel_id=1, source_target_pairs={{28,0},{0,4},{4,8},{8,12},{12,16},{16,20},{20,24},{24,28},{29,1},{... | collective-permute-start | bytes 98312 | tf_op jit(solution)/shard_map/ppermute | solution.py:27
  112.3 8.4 %collective-permute-start.3 = (bf16[16,32,32]{2,1,0:T(8,128)(2,1)S(1)}, bf16[16,32,32]{2,1,0:T(8,128)(2,1)S(1)}, u32[]{:S(2)}, u32[]{:S(2)}) collective-permute-start(bf16[16,32,32]{2,1,0:T(8,128)(2,1)S(1)} %get-tuple-element.6), channel_id=1, source_target_pairs={{4,0},{8,4},{12,8},{16,12},{20,16},{24,20},{28,24},{0,28},{5,1},{9... | collective-permute-start | bytes 98312 | tf_op jit(solution)/shard_map/ppermute | solution.py:27
where the time goes:
time: 129 us; the launch traced here: 128 us
  blocking collectives  64.5 us (50%)
  local copies, waits for them, and re-layouts  32.7 us (25%)
  matrix products  10.8 us (8%)
  starting transfers between devices  9.73 us (8%)
  waiting for transfers between devices  7.88 us (6%)
  other arithmetic  2.53 us (2%)
    unnamed x1, blocking collectives  58.3 us
    gather x1, local copies, waits for them, and re-layouts, level_box(): return lax.dynamic_slice_in_dim(column_block, first, BLEV, 1)  13.1 us
    dot_general x1, local copies, waits for them, and re-layouts, local(): jnp.einsum('ni,cik->nck', row_weight, increment.astype(jnp.float32), prec...  11.5 us
    dot_general x1, matrix products, local(): jnp.einsum('str,sr->st', jacobian, flat_profile, preferred_element_type=j...  6.95 us
    all_gather x1, blocking collectives, local(): packed_all = lax.all_gather(packed, 'lat', axis=0, tiled=True)  6.22 us
    ppermute x1, starting transfers between devices, padded(): lax.ppermute(lax.slice_in_dim(block, 0, width, axis=dim), axis, backward)  4.96 us
    ppermute x2, starting transfers between devices, shifted(): return lax.ppermute(block, axis, route)  4.77 us
    ppermute x1, waiting for transfers between devices, padded(): lax.ppermute(lax.slice_in_dim(block, block.shape[dim] - width, None, axis...  4.52 us
  transfers between devices with their start and end apart: 4, of which 2 were waited for; matrix products, arithmetic and copies ran while one was open for 2% of the time, Pallas kernels for 0%

commit v1 on v0

v1 whole, which is shorter than its diff:
```python
import functools

import jax
import jax.numpy as jnp
from jax import lax
from jax.experimental import pallas as pl
from jax.experimental.pallas import tpu as pltpu
from jax.sharding import PartitionSpec as P

BLAT = 8
BLEV = 32
HALO = 16
MESH = pl.DeviceIdType.MESH


def kernel(
    nlon, nlat, inc_ref, jac_ref, weight_ref, ints_ref, out_ref,
    ext, jbuf, info, sel, shift, pieces, recv,
    inc_sem, jac_sem, halo_send, halo_recv, info_send, info_recv, piece_send, piece_recv,
):
    lon = lax.axis_index("lon")
    lat = lax.axis_index("lat")
    width, rows, lev = inc_ref.shape
    slots, ntan = out_ref.shape
    group = lev // BLEV
    nq = width // group
    depth = rows + HALO
    listed = nlat * slots

    load = pltpu.make_async_copy(inc_ref, ext.at[:, pl.ds(0, rows), :], inc_sem)
    load.start()
    jload = pltpu.make_async_copy(jac_ref, jbuf, jac_sem)
    jload.start()

    def sector(t):
        return lax.rem(lon + t - 1 + nlon, nlon)

    peers = []
    for t in (0, 2, 1):
        for d in range(nlat):
            if t != 1 or d:
                peers.append((t, lax.rem(lat + d, nlat)))

    barrier = pltpu.get_barrier_semaphore()
    for t, l in peers:
        pl.semaphore_signal(barrier, inc=1, device_id=(sector(t), l), device_id_type=MESH)

    eye = lax.broadcasted_iota(jnp.int32, (slots, slots), 0) == lax.broadcasted_iota(
        jnp.int32, (slots, slots), 1
    )

    def column(i):
        row = jnp.broadcast_to(ints_ref[i : i + 1, :].astype(jnp.float32), (slots, slots))
        return jnp.sum(jnp.where(eye, row, 0.0), axis=1, keepdims=True)

    lane = lax.broadcasted_iota(jnp.int32, (slots, lev), 1)
    head = jnp.concatenate(
        [weight_ref[...], jnp.zeros((slots, lev - BLAT), jnp.float32)], axis=1
    )
    head = jnp.where(lane == BLAT, column(3), head)
    head = jnp.where(lane == BLAT + 1, column(4), head)
    info[1, lat] = head
    first = width + column(0) - column(1)
    last = width + column(0) + column(2)

    pl.semaphore_wait(barrier, len(peers))

    def info_copy(t, l):
        return pltpu.make_async_remote_copy(
            src_ref=info.at[1, lat], dst_ref=info.at[2 - t, lat],
            send_sem=info_send.at[t, l], recv_sem=info_recv.at[2 - t, lat],
            device_id=(sector(t), l), device_id_type=MESH,
        )

    for t, l in peers:
        info_copy(t, l).start()
    back = lax.rem(lat + nlat - 1, nlat)
    halo = pltpu.make_async_remote_copy(
        src_ref=inc_ref.at[:, pl.ds(0, HALO), :], dst_ref=ext.at[:, pl.ds(rows, HALO), :],
        send_sem=halo_send, recv_sem=halo_recv,
        device_id=(lon, back), device_id_type=MESH,
    )
    halo.start()

    def info_wait(t, l):
        pltpu.make_async_remote_copy(
            src_ref=info.at[1, lat], dst_ref=info.at[t, l],
            send_sem=info_send.at[t, l], recv_sem=info_recv.at[t, l],
            device_id=(sector(t), l), device_id_type=MESH,
        ).wait_recv()

    def piece_copy(t, l):
        return pltpu.make_async_remote_copy(
            src_ref=pieces.at[t, l], dst_ref=recv.at[2 - t, lat],
            send_sem=piece_send.at[t, l], recv_sem=piece_recv.at[2 - t, lat],
            device_id=(sector(t), l), device_id_type=MESH,
        )

    def piece_wait(t, l):
        pltpu.make_async_remote_copy(
            src_ref=pieces.at[t, l], dst_ref=recv.at[t, l],
            send_sem=piece_send.at[t, l], recv_sem=piece_recv.at[t, l],
            device_id=(sector(t), l), device_id_type=MESH,
        ).wait_recv()

    wide = lax.broadcasted_iota(jnp.int32, (listed, lev), 1)
    base = (lat * rows).astype(jnp.float32)

    ready = False
    for t in (0, 2, 1):
        for s, l in peers:
            if s == t:
                info_wait(t, l)
        table = info[t].reshape(listed, lev)
        local = table[:, BLAT : BLAT + 1] - base
        mine = (local >= 0.0) & (local < float(rows))
        start = jnp.broadcast_to(local, (listed, lev)).astype(jnp.int32)
        mine = jnp.broadcast_to(mine.astype(jnp.int32), (listed, lev)) > 0
        parts = []
        for begin in range(0, depth, lev):
            offset = wide + begin - start
            good = mine & (offset >= 0) & (offset < BLAT)
            picked = jnp.take_along_axis(table, jnp.clip(offset, 0, lev - 1), axis=1)
            parts.append(jnp.where(good, picked, 0.0))
        whole = jnp.concatenate(parts, axis=1)[:, :depth]
        high = whole.astype(jnp.bfloat16)
        low = (whole - high.astype(jnp.float32)).astype(jnp.bfloat16)
        sel[0:listed, :] = high
        sel[listed : 2 * listed, :] = low
        shift[...] = jnp.broadcast_to(table[:, BLAT + 1 : BLAT + 2], (listed, lev)).astype(
            jnp.int32
        ) + lax.rem(wide, BLEV)
        if not ready:
            load.wait()
            halo.wait_recv()
            ready = True

        @pl.loop(0, nq)
        def _(q):
            block = ext[pl.ds(q * group, group)]
            right = jnp.concatenate([block[g] for g in range(group)], axis=1)
            lifted = jnp.dot(sel[...], right, preferred_element_type=jnp.float32)
            lifted = lifted[:listed] + lifted[listed:]
            where = shift[...]
            total = jnp.zeros((listed, lev), jnp.float32)
            for g in range(group):
                moved = jnp.take_along_axis(lifted[:, g * lev : (g + 1) * lev], where, axis=1)
                inside = (wide >= g * BLEV) & (wide < (g + 1) * BLEV)
                total = jnp.where(inside, moved, total)
            total = total.astype(jnp.bfloat16)
            for l in range(nlat):
                pieces[t, l, q] = total[l * slots : (l + 1) * slots]

        for s, l in peers:
            if s == t:
                piece_copy(t, l).start()

    jload.wait()
    span = width * BLEV
    level_row = lax.broadcasted_iota(jnp.int32, (slots, span), 1) // BLEV
    which = lax.broadcasted_iota(jnp.int32, (slots, ntan), 0)
    answer = jnp.zeros((slots, ntan), jnp.float32)
    for t in (1, 0, 2):
        total = None
        if t == 1:
            total = pieces[1, lat].astype(jnp.float32)
        for s, l in peers:
            if s == t:
                piece_wait(t, l)
                value = recv[t, l].astype(jnp.float32)
                total = value if total is None else total + value
        flat = jnp.concatenate([total[q] for q in range(nq)], axis=1)
        at = (level_row + t * width).astype(jnp.float32)
        flat = jnp.where((at >= first) & (at <= last), flat, 0.0).astype(jnp.bfloat16)

        def step(i, answer):
            block = jbuf[pl.ds(2 * i, 2), :, pl.ds(t * span, span)].reshape(2 * ntan, span)
            both = lax.dot_general(
                flat, block, (((1,), (1,)), ((), ())), preferred_element_type=jnp.float32
            )
            answer = answer + jnp.where(which == 2 * i, both[:, :ntan], 0.0)
            return answer + jnp.where(which == 2 * i + 1, both[:, ntan:], 0.0)

        answer = lax.fori_loop(0, slots // 2, step, answer)
    out_ref[...] = answer

    halo.wait_send()
    for t, l in peers:
        info_copy(t, l).wait_send()
        piece_copy(t, l).wait_send()


def local(nlon, nlat, increment, jacobian, lat_weight, centre, west, east, lat_offset, lev_offset):
    width, rows, lev = increment.shape
    slots, ntan, span = jacobian.shape
    nq = width * BLEV // lev
    depth = rows + HALO
    ints = jnp.stack([centre, west, east, lat_offset, lev_offset])
    vmem = pl.BlockSpec(memory_space=pltpu.VMEM)
    hbm = pl.BlockSpec(memory_space=pl.ANY)
    dma = pltpu.SemaphoreType.DMA
    return pl.pallas_call(
        functools.partial(kernel, nlon, nlat),
        out_shape=jax.ShapeDtypeStruct((slots, ntan), jnp.float32),
        in_specs=[hbm, hbm, vmem, vmem],
        out_specs=vmem,
        scratch_shapes=[
            pltpu.VMEM((width, depth, lev), jnp.bfloat16),
            pltpu.VMEM((slots, ntan, span), jnp.bfloat16),
            pltpu.VMEM((3, nlat, slots, lev), jnp.float32),
            pltpu.VMEM((2 * nlat * slots, depth), jnp.bfloat16),
            pltpu.VMEM((nlat * slots, lev), jnp.int32),
            pltpu.VMEM((3, nlat, nq, slots, lev), jnp.bfloat16),
            pltpu.VMEM((3, nlat, nq, slots, lev), jnp.bfloat16),
            dma, dma, dma, dma,
            dma((3, nlat)), dma((3, nlat)), dma((3, nlat)), dma((3, nlat)),
        ],
        compiler_params=pltpu.CompilerParams(
            collective_id=0, has_side_effects=True, vmem_limit_bytes=48 << 20
        ),
    )(increment, jacobian, lat_weight, ints)


def solution(mesh):
    return jax.shard_map(
        functools.partial(local, mesh.shape["lon"], mesh.shape["lat"]),
        mesh=mesh,
        in_specs=(
            P("lon", "lat", None),
            P(("lon", "lat"), None, None),
            P(("lon", "lat"), None),
            P(("lon", "lat")),
            P(("lon", "lat")),
            P(("lon", "lat")),
            P(("lon", "lat")),
            P(("lon", "lat")),
        ),
        out_specs=P(("lon", "lat"), None),
        check_vma=False,
    )
```

time: 129 us -> 31.6 us (0.24)
  blocking collectives: 64.5 us -> 0 us
  local copies, waits for them, and re-layouts: 32.7 us -> 3.32 us
  Pallas kernels: 0 us -> 28 us
  matrix products: 10.8 us -> 0 us
  starting transfers between devices: 9.73 us -> 0 us
  waiting for transfers between devices: 7.88 us -> 0 us
  other arithmetic: 2.53 us -> 0 us
    unnamed x1 -> x0, blocking collectives: 58.3 us -> none
    pallas_call x0 -> x1, Pallas kernels: none -> 28 us  [local(): pl.pallas_call(functools.partial(kernel, nlon, nlat), out_shape=jax.Shape...]
    gather x1 -> x0, local copies, waits for them, and re-layouts: 13.1 us -> none  [level_box(): return lax.dynamic_slice_in_dim(column_block, first, BLEV, 1)]
    dot_general x1 -> x0, local copies, waits for them, and re-layouts: 11.5 us -> none  [local(): jnp.einsum('ni,cik->nck', row_weight, increment.astype(jnp.float32), prec...]
    dot_general x3 -> x0, matrix products: 10.8 us -> none  [the longest x1 6.95 us: local(): jnp.einsum('str,sr->st', jacobian, flat_profile, preferred_element_type=j...]
    ppermute x4 -> x0, starting transfers between devices: 9.73 us -> none  [the longest x1 4.96 us: padded(): lax.ppermute(lax.slice_in_dim(block, 0, width, axis=dim), axis, backward)]
    ppermute x4 -> x0, waiting for transfers between devices: 7.88 us -> none  [the longest x1 4.52 us: padded(): lax.ppermute(lax.slice_in_dim(block, block.shape[dim] - width, None, axis...]
    all_gather x1 -> x0, blocking collectives: 6.22 us -> none  [local(): packed_all = lax.all_gather(packed, 'lat', axis=0, tiled=True)]
  transfers between devices with their start and end apart: 4 -> 0, of which waited for: 2 -> 0; matrix products, arithmetic and copies ran while one was open for 2% -> 0% of each run, Pallas kernels for 0% -> 0%
where the time goes in v1:
time: 31.6 us; the launch traced here: 31.4 us
  Pallas kernels  28 us (89%)
  local copies, waits for them, and re-layouts  3.32 us (11%)
    pallas_call x1, Pallas kernels, local(): pl.pallas_call(functools.partial(kernel, nlon, nlat), out_shape=jax.Shape...  28 us
    unnamed x4, local copies, waits for them, and re-layouts  2.58 us
    another operation x1, local copies, waits for them, and re-layouts, local(): ints = jnp.stack([centre, west, east, lat_offset, lev_offset])  0.74 us

profile of v1, /device:TPU:0, one launch (start us, length us, event | category | flops | bytes accessed | tf_op | source)
XLA Modules:
  0.0 31.4 jit_solution(14261606653158746487)
XLA Ops:
  0.0 0.7 %stack.23.ints_ref = s32[5,16]{1,0:T(8,128)S(1)} concatenate(s32[1,16]{1,0:T(1,128)} %bitcast.5, s32[1,16]{1,0:T(1,128)} %bitcast.6, s32[1,16]{1,0:T(1,128)} %bitcast.7, s32[1,16]{1,0:T(1,128)} %bitcast.8, s32[1,16]{1,0:T(1,128)} %bitcast.9), dimensions={0} | concatenate | bytes 640 | tf_op jit(solution)/shard_map/stack | solution.py:198
  0.7 0.8 %copy.9.weight_ref = f32[16,8]{1,0:T(8,128)S(1)} copy(f32[16,8]{0,1:T(8,128)} %param.10) | data formatting | bytes 1024 | tf_op args[2]
  1.5 0.0 copy-start
  1.5 1.2 %copy-done = bf16[32,128,128]{2,1,0:T(8,128)(2,1)S(1)} copy-done((bf16[32,128,128]{2,1,0:T(8,128)(2,1)S(1)}, bf16[32,128,128]{2,1,0:T(8,128)(2,1)}, u32[]{:S(2)}) %copy-start) | copy-done | bytes 1048600
  2.7 28.0 %shard_map.82 = f32[16,128]{1,0:T(8,128)S(1)} custom-call(bf16[32,128,128]{2,1,0:T(8,128)(2,1)S(1)} %copy-done, bf16[16,128,3072]{2,1,0:T(8,128)(2,1)} %jac_ref.1, f32[16,8]{1,0:T(8,128)S(1)} %copy.9.weight_ref, s32[5,16]{1,0:T(8,128)S(1)} %stack.23.ints_ref), custom_call_target="tpu_custom_call" | custom-call | tf_op jit(solution)/shard_map/pallas_call | solution.py:202
  30.8 0.6 %copy.11 = f32[16,128]{1,0:T(8,128)} copy(f32[16,128]{1,0:T(8,128)S(1)} %shard_map.82) | data formatting | bytes 16384
Async XLA Ops:
  1.5 1.2 %copy-start = (bf16[32,128,128]{2,1,0:T(8,128)(2,1)S(1)}, bf16[32,128,128]{2,1,0:T(8,128)(2,1)}, u32[]{:S(2)}) copy-start(bf16[32,128,128]{2,1,0:T(8,128)(2,1)} %inc_ref.1) | copy-start | bytes 3145732

commit v2 on v1

v2 whole, which is shorter than its diff:
```python
import functools

import jax
import jax.numpy as jnp
from jax import lax
from jax.experimental import pallas as pl
from jax.experimental.pallas import tpu as pltpu
from jax.sharding import PartitionSpec as P

BLAT = 8
BLEV = 32
HALO = 16
MESH = pl.DeviceIdType.MESH


def kernel(
    nlon, nlat, inc_ref, jac_ref, weight_ref, centre_ref, west_ref, east_ref, row_ref, level_ref,
    out_ref, ext, halo, jbuf, info, sel, pieces, recv,
    inc_sem, jac_sem, swap_send, swap_recv, halo_send, halo_recv,
    info_send, info_recv, piece_send, piece_recv,
):
    lon = lax.axis_index("lon")
    lat = lax.axis_index("lat")
    width, rows, lev = inc_ref.shape
    slots, ntan = out_ref.shape
    group = lev // BLEV
    nq = width // group
    part = nq // 2
    half = width // 2
    listed = nlat * slots
    pair = lat // 2
    side = lax.rem(lat, 2)
    npair = nlat // 2

    load = pltpu.make_async_copy(
        inc_ref.at[pl.ds(side * half, half)], ext.at[side], inc_sem
    )
    load.start()
    jload = pltpu.make_async_copy(jac_ref, jbuf, jac_sem)

    def sector(t):
        return lax.rem(lon + t - 1 + nlon, nlon)

    peers = []
    for t in (0, 2, 1):
        for d in range(nlat):
            if t != 1 or d:
                peers.append((t, lax.rem(lat + d, nlat)))

    barrier = pltpu.get_barrier_semaphore()
    for t, l in peers:
        pl.semaphore_signal(barrier, inc=1, device_id=(sector(t), l), device_id_type=MESH)
    jload.start()

    eye = lax.broadcasted_iota(jnp.int32, (slots, slots), 0) == lax.broadcasted_iota(
        jnp.int32, (slots, slots), 1
    )

    def column(row):
        row = jnp.broadcast_to(row.astype(jnp.float32), (slots, slots))
        return jnp.sum(jnp.where(eye, row, 0.0), axis=1, keepdims=True)

    lane = lax.broadcasted_iota(jnp.int32, (slots, lev), 1)
    head = jnp.zeros((slots, lev), jnp.float32)
    for j in range(BLAT):
        head = jnp.where(lane == j, column(weight_ref[j : j + 1, :]), head)
    head = jnp.where(lane == BLAT, column(row_ref[...]), head)
    head = jnp.where(lane == BLAT + 1, column(level_ref[...]), head)
    info[1, lat] = head
    middle = width + column(centre_ref[...])
    first = middle - column(west_ref[...])
    last = middle + column(east_ref[...])

    pl.semaphore_wait(barrier, len(peers))

    def info_copy(t, l):
        return pltpu.make_async_remote_copy(
            src_ref=info.at[1, lat], dst_ref=info.at[2 - t, lat],
            send_sem=info_send.at[t, l], recv_sem=info_recv.at[2 - t, lat],
            device_id=(sector(t), l), device_id_type=MESH,
        )

    for t, l in peers:
        info_copy(t, l).start()
    swap = pltpu.make_async_remote_copy(
        src_ref=inc_ref.at[pl.ds((1 - side) * half, half)], dst_ref=ext.at[side],
        send_sem=swap_send, recv_sem=swap_recv,
        device_id=(lon, pair * 2 + 1 - side), device_id_type=MESH,
    )

    def halo_copy(other):
        return pltpu.make_async_remote_copy(
            src_ref=inc_ref.at[pl.ds(other * half, half), pl.ds(0, HALO), :], dst_ref=halo,
            send_sem=halo_send.at[other], recv_sem=halo_recv,
            device_id=(lon, lax.rem(pair + npair - 1, npair) * 2 + other), device_id_type=MESH,
        )

    @pl.when(side == 0)
    def _():
        halo_copy(0).start()
        halo_copy(1).start()

    swap.start()

    def info_wait(t, l):
        pltpu.make_async_remote_copy(
            src_ref=info.at[1, lat], dst_ref=info.at[t, l],
            send_sem=info_send.at[t, l], recv_sem=info_recv.at[t, l],
            device_id=(sector(t), l), device_id_type=MESH,
        ).wait_recv()

    def slot(u, l):
        return recv.at[u, l // 2, pl.ds(lax.rem(l, 2) * part, part)]

    def piece_copy(t, l):
        return pltpu.make_async_remote_copy(
            src_ref=pieces.at[t, l], dst_ref=slot(2 - t, lat),
            send_sem=piece_send.at[t, l], recv_sem=piece_recv.at[2 - t, lat],
            device_id=(sector(t), l), device_id_type=MESH,
        )

    def piece_wait(t, l):
        pltpu.make_async_remote_copy(
            src_ref=pieces.at[t, l], dst_ref=slot(t, l),
            send_sem=piece_send.at[t, l], recv_sem=piece_recv.at[t, l],
            device_id=(sector(t), l), device_id_type=MESH,
        ).wait_recv()

    depth = 2 * rows + HALO
    wide = lax.broadcasted_iota(jnp.int32, (listed, lev), 1)
    base = (pair * 2 * rows).astype(jnp.float32)

    ready = False
    for t in (0, 2, 1):
        for s, l in peers:
            if s == t:
                info_wait(t, l)
        table = info[t].reshape(listed, lev)
        local = table[:, BLAT : BLAT + 1] - base
        mine = (local >= 0.0) & (local < float(2 * rows))
        start = jnp.broadcast_to(local, (listed, lev)).astype(jnp.int32)
        mine = jnp.broadcast_to(mine.astype(jnp.int32), (listed, lev)) > 0
        parts = []
        for begin in range(0, depth, lev):
            offset = wide + begin - start
            good = mine & (offset >= 0) & (offset < BLAT)
            picked = jnp.take_along_axis(table, jnp.clip(offset, 0, lev - 1), axis=1)
            parts.append(jnp.where(good, picked, 0.0))
        whole = jnp.concatenate(parts, axis=1)[:, :depth]
        high = whole.astype(jnp.bfloat16)
        low = (whole - high.astype(jnp.float32)).astype(jnp.bfloat16)
        sel[0:listed, :] = high
        sel[listed : 2 * listed, :] = low
        where = jnp.broadcast_to(table[:, BLAT + 1 : BLAT + 2], (listed, lev)).astype(
            jnp.int32
        ) + lax.rem(wide, BLEV)
        if not ready:
            load.wait()
            swap.wait_recv()
            halo_copy(0).wait_recv()
            ready = True

        for q in range(part):
            right = jnp.concatenate(
                [
                    jnp.concatenate(
                        [ext[0, q * group + g], ext[1, q * group + g], halo[q * group + g]], axis=0
                    )
                    for g in range(group)
                ],
                axis=1,
            )
            lifted = jnp.dot(sel[...], right, preferred_element_type=jnp.float32)
            lifted = lifted[:listed] + lifted[listed:]
            total = jnp.zeros((listed, lev), jnp.float32)
            for g in range(group):
                moved = jnp.take_along_axis(lifted[:, g * lev : (g + 1) * lev], where, axis=1)
                inside = (wide >= g * BLEV) & (wide < (g + 1) * BLEV)
                total = jnp.where(inside, moved, total)
            total = total.astype(jnp.bfloat16)
            for l in range(nlat):
                pieces[t, l, q] = total[l * slots : (l + 1) * slots]

        for s, l in peers:
            if s == t:
                piece_copy(t, l).start()

    keep = pltpu.make_async_copy(pieces.at[1, lat], slot(1, lat), inc_sem)
    keep.start()
    jload.wait()
    keep.wait()
    span = width * BLEV
    level_row = lax.broadcasted_iota(jnp.int32, (slots, span), 1) // BLEV
    which = lax.broadcasted_iota(jnp.int32, (slots, ntan), 0)
    answer = jnp.zeros((slots, ntan), jnp.float32)
    for t in (1, 0, 2):
        for s, l in peers:
            if s == t:
                piece_wait(t, l)
        total = recv[t, 0].astype(jnp.float32)
        for p in range(1, npair):
            total = total + recv[t, p].astype(jnp.float32)
        flat = jnp.concatenate([total[q] for q in range(nq)], axis=1)
        at = (level_row + t * width).astype(jnp.float32)
        flat = jnp.where((at >= first) & (at <= last), flat, 0.0).astype(jnp.bfloat16)

        def step(i, answer):
            block = jbuf[pl.ds(2 * i, 2), :, pl.ds(t * span, span)].reshape(2 * ntan, span)
            both = lax.dot_general(
                flat, block, (((1,), (1,)), ((), ())), preferred_element_type=jnp.float32
            )
            answer = answer + jnp.where(which == 2 * i, both[:, :ntan], 0.0)
            return answer + jnp.where(which == 2 * i + 1, both[:, ntan:], 0.0)

        answer = lax.fori_loop(0, slots // 2, step, answer)
    out_ref[...] = answer

    swap.wait_send()

    @pl.when(side == 0)
    def _():
        halo_copy(0).wait_send()
        halo_copy(1).wait_send()

    for t, l in peers:
        info_copy(t, l).wait_send()
        piece_copy(t, l).wait_send()


def local(nlon, nlat, increment, jacobian, lat_weight, centre, west, east, lat_offset, lev_offset):
    width, rows, lev = increment.shape
    slots, ntan, span = jacobian.shape
    nq = width * BLEV // lev
    vmem = pl.BlockSpec(memory_space=pltpu.VMEM)
    hbm = pl.BlockSpec(memory_space=pltpu.HBM)
    dma = pltpu.SemaphoreType.DMA
    ints = [v.reshape(1, slots) for v in (centre, west, east, lat_offset, lev_offset)]
    return pl.pallas_call(
        functools.partial(kernel, nlon, nlat),
        out_shape=jax.ShapeDtypeStruct((slots, ntan), jnp.float32),
        in_specs=[hbm, hbm] + [vmem] * 6,
        out_specs=vmem,
        scratch_shapes=[
            pltpu.VMEM((2, width // 2, rows, lev), jnp.bfloat16),
            pltpu.VMEM((width // 2, HALO, lev), jnp.bfloat16),
            pltpu.VMEM((slots, ntan, span), jnp.bfloat16),
            pltpu.VMEM((3, nlat, slots, lev), jnp.float32),
            pltpu.VMEM((2 * nlat * slots, 2 * rows + HALO), jnp.bfloat16),
            pltpu.VMEM((3, nlat, nq // 2, slots, lev), jnp.bfloat16),
            pltpu.VMEM((3, nlat // 2, nq, slots, lev), jnp.bfloat16),
            dma, dma, dma, dma, dma((2,)), dma,
            dma((3, nlat)), dma((3, nlat)), dma((3, nlat)), dma((3, nlat)),
        ],
        compiler_params=pltpu.CompilerParams(
            collective_id=0, has_side_effects=True, vmem_limit_bytes=56 << 20
        ),
    )(increment, jacobian, lat_weight.T, *ints)


def solution(mesh):
    return jax.shard_map(
        functools.partial(local, mesh.shape["lon"], mesh.shape["lat"]),
        mesh=mesh,
        in_specs=(
            P("lon", "lat", None),
            P(("lon", "lat"), None, None),
            P(("lon", "lat"), None),
            P(("lon", "lat")),
            P(("lon", "lat")),
            P(("lon", "lat")),
            P(("lon", "lat")),
            P(("lon", "lat")),
        ),
        out_specs=P(("lon", "lat"), None),
        check_vma=False,
    )
```

time: 31.6 us -> 25 us (0.79)
  Pallas kernels: 28 us -> 23.5 us
  local copies, waits for them, and re-layouts: 3.32 us -> 1.3 us
    pallas_call x1, Pallas kernels: 28 us -> 23.5 us  [local(): pl.pallas_call(functools.partial(kernel, nlon, nlat), out_shape=jax.Shape...]
    unnamed x4 -> x1, local copies, waits for them, and re-layouts: 2.58 us -> 1.3 us
    another operation x1 -> x0, local copies, waits for them, and re-layouts: 0.74 us -> none  [local(): ints = jnp.stack([centre, west, east, lat_offset, lev_offset])]
where the time goes in v2:
time: 25 us; the launch traced here: 24.8 us
  Pallas kernels  23.5 us (94%)
  local copies, waits for them, and re-layouts  1.3 us (5%)
    pallas_call x1, Pallas kernels, local(): pl.pallas_call(functools.partial(kernel, nlon, nlat), out_shape=jax.Shape...  23.5 us
    unnamed x1, local copies, waits for them, and re-layouts  1.3 us

profile of v2, /device:TPU:0, one launch (start us, length us, event | category | flops | bytes accessed | tf_op | source)
XLA Modules:
  0.0 24.8 jit_solution(12495042515996225370)
XLA Ops:
  0.0 23.5 %shard_map.82 = f32[16,128]{1,0:T(8,128)} custom-call(bf16[32,128,128]{2,1,0:T(8,128)(2,1)} %inc_ref.1, bf16[16,128,3072]{2,1,0:T(8,128)(2,1)} %jac_ref.1, f32[8,16]{1,0:T(8,128)} %bitcast.6, s32[1,16]{1,0:T(1,128)} %bitcast.7, s32[1,16]{1,0:T(1,128)} %bitcast.8, s32[1,16]{1,0:T(1,128)} %bitcast.9, s32[1,16]{1,0:T(1,128)} %bitcast.10, s32[1,16]{1,0:T(1,128)} %bitcast.11), custom_call_target="tpu_custom_call" | custom-call | tf_op jit(solution)/shard_map/pallas_call | solution.py:238
  23.5 1.3 %copy.10 = f32[16,128]{1,0:T(8,128)} copy(f32[16,128]{1,0:T(8,128)} %shard_map.82) | data formatting | bytes 16384

commit v3 on v2

--- a/solution.py
+++ b/solution.py
@@ -9,7 +9,8 @@
 
 BLAT = 8
 BLEV = 32
-HALO = 16
+HALO = 8
+FIELDS = 16
 MESH = pl.DeviceIdType.MESH
 
 
@@ -28,6 +29,7 @@
     part = nq // 2
     half = width // 2
     listed = nlat * slots
+    packed = lev // FIELDS
     pair = lat // 2
     side = lax.rem(lat, 2)
     npair = nlat // 2
@@ -66,7 +68,16 @@
         head = jnp.where(lane == j, column(weight_ref[j : j + 1, :]), head)
     head = jnp.where(lane == BLAT, column(row_ref[...]), head)
     head = jnp.where(lane == BLAT + 1, column(level_ref[...]), head)
-    info[1, lat] = head
+    place = lax.broadcasted_iota(jnp.int32, (slots, lev), 0)
+    spread = jnp.take_along_axis(head, lax.rem(lane, FIELDS), axis=1)
+    spread = jnp.where(lane // FIELDS == lax.rem(place, packed), spread, 0.0)
+    info[1, lat] = jnp.concatenate(
+        [
+            jnp.sum(spread[r * packed : (r + 1) * packed], axis=0, keepdims=True)
+            for r in range(slots // packed)
+        ],
+        axis=0,
+    )
     middle = width + column(centre_ref[...])
     first = middle - column(west_ref[...])
     last = middle + column(east_ref[...])
@@ -128,14 +139,25 @@
 
     depth = 2 * rows + HALO
     wide = lax.broadcasted_iota(jnp.int32, (listed, lev), 1)
+    unpack = lax.rem(
+        lax.rem(lax.broadcasted_iota(jnp.int32, (listed, lev), 0), packed) * FIELDS + wide, lev
+    )
     base = (pair * 2 * rows).astype(jnp.float32)
 
     ready = False
-    for t in (0, 2, 1):
+    for t in (1, 0, 2):
         for s, l in peers:
             if s == t:
                 info_wait(t, l)
-        table = info[t].reshape(listed, lev)
+        table = jnp.concatenate(
+            [
+                jnp.broadcast_to(info[t, l, r : r + 1, :], (packed, lev))
+                for l in range(nlat)
+                for r in range(slots // packed)
+            ],
+            axis=0,
+        )
+        table = jnp.take_along_axis(table, unpack, axis=1)
         local = table[:, BLAT : BLAT + 1] - base
         mine = (local >= 0.0) & (local < float(2 * rows))
         start = jnp.broadcast_to(local, (listed, lev)).astype(jnp.int32)
@@ -193,7 +215,7 @@
     level_row = lax.broadcasted_iota(jnp.int32, (slots, span), 1) // BLEV
     which = lax.broadcasted_iota(jnp.int32, (slots, ntan), 0)
     answer = jnp.zeros((slots, ntan), jnp.float32)
-    for t in (1, 0, 2):
+    for t in (1, 2, 0):
         for s, l in peers:
             if s == t:
                 piece_wait(t, l)
@@ -204,15 +226,13 @@
         at = (level_row + t * width).astype(jnp.float32)
         flat = jnp.where((at >= first) & (at <= last), flat, 0.0).astype(jnp.bfloat16)
 
-        def step(i, answer):
-            block = jbuf[pl.ds(2 * i, 2), :, pl.ds(t * span, span)].reshape(2 * ntan, span)
+        for i in range(slots // 2):
+            block = jbuf[2 * i : 2 * i + 2, :, t * span : (t + 1) * span].reshape(2 * ntan, span)
             both = lax.dot_general(
                 flat, block, (((1,), (1,)), ((), ())), preferred_element_type=jnp.float32
             )
             answer = answer + jnp.where(which == 2 * i, both[:, :ntan], 0.0)
-            return answer + jnp.where(which == 2 * i + 1, both[:, ntan:], 0.0)
-
-        answer = lax.fori_loop(0, slots // 2, step, answer)
+            answer = answer + jnp.where(which == 2 * i + 1, both[:, ntan:], 0.0)
     out_ref[...] = answer
 
     swap.wait_send()
@@ -244,7 +264,7 @@
             pltpu.VMEM((2, width // 2, rows, lev), jnp.bfloat16),
             pltpu.VMEM((width // 2, HALO, lev), jnp.bfloat16),
             pltpu.VMEM((slots, ntan, span), jnp.bfloat16),
-            pltpu.VMEM((3, nlat, slots, lev), jnp.float32),
+            pltpu.VMEM((3, nlat, slots * FIELDS // lev, lev), jnp.float32),
             pltpu.VMEM((2 * nlat * slots, 2 * rows + HALO), jnp.bfloat16),
             pltpu.VMEM((3, nlat, nq // 2, slots, lev), jnp.bfloat16),
             pltpu.VMEM((3, nlat // 2, nq, slots, lev), jnp.bfloat16),

time: 25 us -> 21.7 us (0.87)
  Pallas kernels: 23.5 us -> 20.2 us
    pallas_call x1, Pallas kernels: 23.5 us -> 20.2 us  [local(): pl.pallas_call(functools.partial(kernel, nlon, nlat), out_shape=jax.Shape...]
where the time goes in v3:
time: 21.7 us; the launch traced here: 21.5 us
  Pallas kernels  20.2 us (93%)
  local copies, waits for them, and re-layouts  1.3 us (6%)
    pallas_call x1, Pallas kernels, local(): pl.pallas_call(functools.partial(kernel, nlon, nlat), out_shape=jax.Shape...  20.2 us
    unnamed x1, local copies, waits for them, and re-layouts  1.3 us

profile of v3, /device:TPU:0, one launch (start us, length us, event | category | flops | bytes accessed | tf_op | source)
XLA Modules:
  0.0 21.5 jit_solution(14637806020100534954)
XLA Ops:
  0.0 20.2 %shard_map.82 = f32[16,128]{1,0:T(8,128)} custom-call(bf16[32,128,128]{2,1,0:T(8,128)(2,1)} %inc_ref.1, bf16[16,128,3072]{2,1,0:T(8,128)(2,1)} %jac_ref.1, f32[8,16]{1,0:T(8,128)} %bitcast.6, s32[1,16]{1,0:T(1,128)} %bitcast.7, s32[1,16]{1,0:T(1,128)} %bitcast.8, s32[1,16]{1,0:T(1,128)} %bitcast.9, s32[1,16]{1,0:T(1,128)} %bitcast.10, s32[1,16]{1,0:T(1,128)} %bitcast.11), custom_call_target="tpu_custom_call" | custom-call | tf_op jit(solution)/shard_map/pallas_call | solution.py:258
  20.2 1.3 %copy.10 = f32[16,128]{1,0:T(8,128)} copy(f32[16,128]{1,0:T(8,128)} %shard_map.82) | data formatting | bytes 16384

commit v4 on v3

--- a/solution.py
+++ b/solution.py
@@ -15,8 +15,9 @@
 
 
 def kernel(
-    nlon, nlat, inc_ref, jac_ref, weight_ref, centre_ref, west_ref, east_ref, row_ref, level_ref,
-    out_ref, ext, halo, jbuf, info, sel, pieces, recv,
+    nlon, nlat, inc_ref, jac_ref, weight_hbm, centre_hbm, west_hbm, east_hbm, row_hbm, level_hbm,
+    out_ref, weight_ref, centre_ref, west_ref, east_ref, row_ref, level_ref, small_sem,
+    ext, halo, jbuf, info, sel, pieces, recv,
     inc_sem, jac_sem, swap_send, swap_recv, halo_send, halo_recv,
     info_send, info_recv, piece_send, piece_recv,
 ):
@@ -37,7 +38,6 @@
     load = pltpu.make_async_copy(
         inc_ref.at[pl.ds(side * half, half)], ext.at[side], inc_sem
     )
-    load.start()
     jload = pltpu.make_async_copy(jac_ref, jbuf, jac_sem)
 
     def sector(t):
@@ -52,6 +52,18 @@
     barrier = pltpu.get_barrier_semaphore()
     for t, l in peers:
         pl.semaphore_signal(barrier, inc=1, device_id=(sector(t), l), device_id_type=MESH)
+    small = [
+        pltpu.make_async_copy(source, target, small_sem.at[i])
+        for i, (source, target) in enumerate(
+            [
+                (weight_hbm, weight_ref), (row_hbm, row_ref), (level_hbm, level_ref),
+                (centre_hbm, centre_ref), (west_hbm, west_ref), (east_hbm, east_ref),
+            ]
+        )
+    ]
+    for copy in small:
+        copy.start()
+    load.start()
     jload.start()
 
     eye = lax.broadcasted_iota(jnp.int32, (slots, slots), 0) == lax.broadcasted_iota(
@@ -62,6 +74,8 @@
         row = jnp.broadcast_to(row.astype(jnp.float32), (slots, slots))
         return jnp.sum(jnp.where(eye, row, 0.0), axis=1, keepdims=True)
 
+    for copy in small:
+        copy.wait()
     lane = lax.broadcasted_iota(jnp.int32, (slots, lev), 1)
     head = jnp.zeros((slots, lev), jnp.float32)
     for j in range(BLAT):
@@ -257,10 +271,13 @@
     ints = [v.reshape(1, slots) for v in (centre, west, east, lat_offset, lev_offset)]
     return pl.pallas_call(
         functools.partial(kernel, nlon, nlat),
-        out_shape=jax.ShapeDtypeStruct((slots, ntan), jnp.float32),
-        in_specs=[hbm, hbm] + [vmem] * 6,
+        out_shape=pltpu.VMEM((slots, ntan), jnp.float32),
+        in_specs=[hbm] * 8,
         out_specs=vmem,
         scratch_shapes=[
+            pltpu.VMEM((BLAT, slots), jnp.float32),
+            *[pltpu.VMEM((1, slots), jnp.int32)] * 5,
+            dma((6,)),
             pltpu.VMEM((2, width // 2, rows, lev), jnp.bfloat16),
             pltpu.VMEM((width // 2, HALO, lev), jnp.bfloat16),
             pltpu.VMEM((slots, ntan, span), jnp.bfloat16),

time: 21.7 us -> 19.7 us (0.908)
  Pallas kernels: 20.2 us -> 18.9 us
  local copies, waits for them, and re-layouts: 1.3 us -> 0.6 us
    pallas_call x1, Pallas kernels: 20.2 us -> 18.9 us  [local(): pl.pallas_call(functools.partial(kernel, nlon, nlat), out_shape=pltpu.VME...]
    unnamed x1, local copies, waits for them, and re-layouts: 1.3 us -> 0.6 us
where the time goes in v4:
time: 19.7 us; the launch traced here: 19.5 us
  Pallas kernels  18.9 us (96%)
  local copies, waits for them, and re-layouts  0.6 us (3%)
    pallas_call x1, Pallas kernels, local(): pl.pallas_call(functools.partial(kernel, nlon, nlat), out_shape=pltpu.VME...  18.9 us
    unnamed x1, local copies, waits for them, and re-layouts  0.6 us

profile of v4, /device:TPU:0, one launch (start us, length us, event | category | flops | bytes accessed | tf_op | source)
XLA Modules:
  0.0 19.5 jit_solution(18044901041980445334)
XLA Ops:
  0.0 18.9 %shard_map.82 = f32[16,128]{1,0:T(8,128)S(1)} custom-call(bf16[32,128,128]{2,1,0:T(8,128)(2,1)} %inc_ref.1, bf16[16,128,3072]{2,1,0:T(8,128)(2,1)} %jac_ref.1, f32[8,16]{1,0:T(8,128)} %bitcast.6, s32[1,16]{1,0:T(1,128)} %bitcast.7, s32[1,16]{1,0:T(1,128)} %bitcast.8, s32[1,16]{1,0:T(1,128)} %bitcast.9, s32[1,16]{1,0:T(1,128)} %bitcast.10, s32[1,16]{1,0:T(1,128)} %bitcast.11), custom_call_target="tpu_custom_call" | custom-call | tf_op jit(solution)/shard_map/pallas_call | solution.py:272
  18.9 0.6 %copy.10 = f32[16,128]{1,0:T(8,128)} copy(f32[16,128]{1,0:T(8,128)S(1)} %shard_map.82) | data formatting | bytes 16384

commit v5 on v4

--- a/solution.py
+++ b/solution.py
@@ -74,7 +74,7 @@
         row = jnp.broadcast_to(row.astype(jnp.float32), (slots, slots))
         return jnp.sum(jnp.where(eye, row, 0.0), axis=1, keepdims=True)
 
-    for copy in small:
+    for copy in small[:3]:
         copy.wait()
     lane = lax.broadcasted_iota(jnp.int32, (slots, lev), 1)
     head = jnp.zeros((slots, lev), jnp.float32)
@@ -92,9 +92,6 @@
         ],
         axis=0,
     )
-    middle = width + column(centre_ref[...])
-    first = middle - column(west_ref[...])
-    last = middle + column(east_ref[...])
 
     pl.semaphore_wait(barrier, len(peers))
 
@@ -126,6 +123,11 @@
         halo_copy(1).start()
 
     swap.start()
+    for copy in small[3:]:
+        copy.wait()
+    middle = width + column(centre_ref[...])
+    first = middle - column(west_ref[...])
+    last = middle + column(east_ref[...])
 
     def info_wait(t, l):
         pltpu.make_async_remote_copy(

time: 19.7 us -> 19.7 us (level)
  no operation moved by 1% of the time
where the time goes in v5:
time: 19.7 us; the launch traced here: 19.5 us
  Pallas kernels  18.9 us (96%)
  local copies, waits for them, and re-layouts  0.6 us (3%)
    pallas_call x1, Pallas kernels, local(): pl.pallas_call(functools.partial(kernel, nlon, nlat), out_shape=pltpu.VME...  18.9 us
    unnamed x1, local copies, waits for them, and re-layouts  0.6 us

profile of v5, /device:TPU:0, one launch (start us, length us, event | category | flops | bytes accessed | tf_op | source)
XLA Modules:
  0.0 19.5 jit_solution(16353767385835651238)
XLA Ops:
  0.0 18.9 %shard_map.82 = f32[16,128]{1,0:T(8,128)S(1)} custom-call(bf16[32,128,128]{2,1,0:T(8,128)(2,1)} %inc_ref.1, bf16[16,128,3072]{2,1,0:T(8,128)(2,1)} %jac_ref.1, f32[8,16]{1,0:T(8,128)} %bitcast.6, s32[1,16]{1,0:T(1,128)} %bitcast.7, s32[1,16]{1,0:T(1,128)} %bitcast.8, s32[1,16]{1,0:T(1,128)} %bitcast.9, s32[1,16]{1,0:T(1,128)} %bitcast.10, s32[1,16]{1,0:T(1,128)} %bitcast.11), custom_call_target="tpu_custom_call" | custom-call | tf_op jit(solution)/shard_map/pallas_call | solution.py:274
  18.9 0.6 %copy.10 = f32[16,128]{1,0:T(8,128)} copy(f32[16,128]{1,0:T(8,128)S(1)} %shard_map.82) | data formatting | bytes 16384
